TPU v7x, 256 devices: a whole 4x4x8 slice. The times are simulated.
256 devices in a mesh: row: 8 (over z_hi, y), col: 32 (over x, z_lo, core).
Axes of the slice: x: 4, y: 4, z: 8 (z_hi: 2, z_lo: 4; z = z_hi * 4 + z_lo), core: 2. Of those that a mesh axis runs over, the one named last changes fastest.
Arguments:
- features: bfloat16 [65536, 256], P('col', 'row'), may hold values from -6 to 6
- block_values: bfloat16 [8, 32, 256, 128, 128], P('row', 'col'), may hold values from -0.046875 to 0.046875
- block_coords: int32 [8, 32, 2, 256], P('row', 'col'), may hold values from 0 to 63, as said below
- live_blocks: int32 [8, 32], P('row', 'col'), may hold values from 32 to 256, as said below
- weight: bfloat16 [256, 256], replicated, may hold values from -0.375 to 0.375
- bias: float32 [256], replicated, may hold values from -3 to 3
- cotangent: bfloat16 [65536, 256], P(('row', 'col')), may hold values from -6 to 6
Outputs:
- out: bfloat16 [65536, 256], P(('row', 'col'))
- grad_x: bfloat16 [65536, 256], P('col', 'row')
- grad_weight: float32 [256, 256], replicated
- grad_bias: float32 [256], replicated
Inputs may be any that keep to these rules, and one draw needn't show every extreme that they name: `block_coords`: within one tile the 256 slots name distinct pairs of a row block (0 to 63) and a column block (0 to 15). Only the first live_blocks[i, j] slots of tile (i, j) belong to the adjacency; some tile has all 256 slots live.
All inputs are finite; a program needn't handle non-finite values.
Results may differ from a plain program's by a relative error of at most 0.0075.
Values may be sent and summed in bfloat16 or wider, within the bound.
A program may use at most 128 MiB of HBM per device.

v0:
```python
import math
import jax
import jax.numpy as jnp
from jax import lax
from jax.sharding import PartitionSpec as P


def block_products(block_vals, source, dst_index, src_index, live_count, out_blocks, transposed):
    slot_total = block_vals.shape[0]
    block_size = block_vals.shape[1]
    feat_width = source.shape[2]
    group_size = math.gcd(slot_total, 64)
    pattern = "sab,saf->sbf" if transposed else "sab,sbf->saf"
    offsets = jnp.arange(group_size, dtype=jnp.int32)

    def one_group(turn, totals):
        first_slot = turn * group_size
        slab_vals = lax.dynamic_slice_in_dim(block_vals, first_slot, group_size, 0)
        take_from = lax.dynamic_slice_in_dim(src_index, first_slot, group_size, 0)
        put_to = lax.dynamic_slice_in_dim(dst_index, first_slot, group_size, 0)
        picked = jnp.take(source, take_from, axis=0)
        products = jnp.einsum(pattern, slab_vals, picked, preferred_element_type=jnp.float32)
        alive_mask = first_slot + offsets < live_count
        products = jnp.where(alive_mask[:, None, None], products, 0.0)
        return totals.at[put_to].add(products)

    start_totals = jnp.zeros((out_blocks, block_size, feat_width), jnp.float32)
    turns = slot_total // group_size
    return lax.fori_loop(0, turns, one_group, start_totals)


def on_device(features, block_values, block_coords, live_blocks, weight, bias, cotangent):
    block_vals = block_values[0, 0]
    row_ids = block_coords[0, 0, 0]
    col_ids = block_coords[0, 0, 1]
    live_count = live_blocks[0, 0]
    block_size = block_vals.shape[1]
    feat_width = weight.shape[0]
    col_count = lax.axis_size("col")
    feat_tile = lax.all_gather(features, "row", axis=1, tiled=True)
    col_blocks = feat_tile.shape[0] // block_size
    row_blocks = cotangent.shape[0] * col_count // block_size
    feat_blocks = feat_tile.reshape(col_blocks, block_size, feat_width)
    partial_value = block_products(
        block_vals, feat_blocks, row_ids, col_ids, live_count, row_blocks, False
    )
    partial_value = partial_value.reshape(row_blocks * block_size, feat_width)
    aggregate = lax.psum_scatter(partial_value, "col", scatter_dimension=0, tiled=True).astype(
        jnp.bfloat16
    )
    preact = jnp.dot(aggregate, weight, preferred_element_type=jnp.float32) + bias
    sigmoid_v = jax.nn.sigmoid(preact)
    out = (preact * sigmoid_v).astype(jnp.bfloat16)
    derivative = sigmoid_v * (1.0 + preact * (1.0 - sigmoid_v))
    grad_pre = (cotangent.astype(jnp.float32) * derivative).astype(jnp.bfloat16)
    weight_term = lax.dot_general(
        aggregate, grad_pre, (((0,), (0,)), ((), ())), preferred_element_type=jnp.float32
    )
    bias_term = jnp.sum(grad_pre.astype(jnp.float32), axis=0)
    weight_sum, bias_sum = lax.psum((weight_term, bias_term), ("row", "col"))
    norm_factor = (feat_tile.shape[0] * col_count) ** (-0.5)
    grad_weight = weight_sum * norm_factor
    grad_bias = bias_sum * norm_factor
    grad_agg = lax.dot_general(
        grad_pre, weight, (((1,), (1,)), ((), ())), preferred_element_type=jnp.float32
    ).astype(jnp.bfloat16)
    grad_tile = lax.all_gather(grad_agg, "col", axis=0, tiled=True)
    grad_blocks = grad_tile.reshape(row_blocks, block_size, feat_width)
    partial_x = block_products(
        block_vals, grad_blocks, col_ids, row_ids, live_count, col_blocks, True
    )
    partial_x = partial_x.reshape(col_blocks * block_size, feat_width)
    grad_x = lax.psum_scatter(partial_x, "row", scatter_dimension=1, tiled=True).astype(
        jnp.bfloat16
    )
    return (out, grad_x, grad_weight, grad_bias)


def solution(mesh):
    in_specs = (
        P("col", "row"),
        P("row", "col", None, None, None),
        P("row", "col", None, None),
        P("row", "col"),
        P(),
        P(),
        P(("row", "col"), None),
    )
    out_specs = (P(("row", "col"), None), P("col", "row"), P(), P())
    return jax.shard_map(
        on_device, mesh=mesh, in_specs=in_specs, out_specs=out_specs, check_vma=False
    )
```

profile of v0, /device:TPU:2, one launch (start us, length us, event | category | flops | bytes accessed | tf_op | source)
XLA Modules:
  0.0 785.1 jit_solution(2173765968436024874)
XLA Ops:
  8.7 66.8 %all-gather.3.cloned.1.call-done = bf16[2048,256]{0,1:T(8,128)(2,1)} async-done(((bf16[2048,32]{0,1:T(8,128)(2,1)}), bf16[2048,256]{0,1:T(8,128)(2,1)}) %all-gather.3.cloned.1.call-update) | async-done | bytes 1048592 | tf_op jit(solution)/shard_map/all_gather | solution.py:40
  81.3 122.0 %while.28 = (s32[]{:T(128)}, f32[64,128,256]{2,1,0:T(8,128)}, s32[256]{0:T(256)S(1)}, s32[]{:T(128)}, bf16[256,128,128]{2,1,0:T(8,128)(2,1)}, /*index=5*/s32[256...) while((s32[]{:T(128)}, f32[64,128,256]{2,1,0:T(8,128)}, ...), condition=%wide.region_2.3_spmd.clone, body=%wide.region_0.2_spmd.clone.sunk | while | flops 543164096 | bytes 48240816 | solution.py:29
  84.8 7.4 broadcast_select_fusion.4
  92.2 19.6 %scatter_fusion = f32[64,128,256]{2,1,0:T(8,128)} fusion(f32[64,128,256]{2,1,0:T(8,128)} %get-tuple-element.472, s32[64]{0:T(128)S(1)} %compare_select_fusion.8, f32[64,128,256]{2,1,0:T(8,128)} %broadcast_select_fusion.4), kind=kCustom, calls=%fused_computation.2.clone.clone.1 | custom fusion | flops 2097152 | bytes 25166080 | tf_op jit(solution)/shard_map/while/body/eval_jaxpr/scatter-add | solution.py:25
  122.8 19.4 %scatter_fusion = f32[64,128,256]{2,1,0:T(8,128)} fusion(f32[64,128,256]{2,1,0:T(8,128)} %get-tuple-element.472, s32[64]{0:T(128)S(1)} %compare_select_fusion.8, f32[64,128,256]{2,1,0:T(8,128)} %broadcast_select_fusion.4), kind=kCustom, calls=%fused_computation.2.clone.clone.1 | custom fusion | flops 2097152 | bytes 25166080 | tf_op jit(solution)/shard_map/while/body/eval_jaxpr/scatter-add | solution.py:25
  145.7 7.4 broadcast_select_fusion.4
  153.1 19.6 %scatter_fusion = f32[64,128,256]{2,1,0:T(8,128)} fusion(f32[64,128,256]{2,1,0:T(8,128)} %get-tuple-element.472, s32[64]{0:T(128)S(1)} %compare_select_fusion.8, f32[64,128,256]{2,1,0:T(8,128)} %broadcast_select_fusion.4), kind=kCustom, calls=%fused_computation.2.clone.clone.1 | custom fusion | flops 2097152 | bytes 25166080 | tf_op jit(solution)/shard_map/while/body/eval_jaxpr/scatter-add | solution.py:25
  176.2 7.4 broadcast_select_fusion.4
  183.6 19.6 %scatter_fusion = f32[64,128,256]{2,1,0:T(8,128)} fusion(f32[64,128,256]{2,1,0:T(8,128)} %get-tuple-element.472, s32[64]{0:T(128)S(1)} %compare_select_fusion.8, f32[64,128,256]{2,1,0:T(8,128)} %broadcast_select_fusion.4), kind=kCustom, calls=%fused_computation.2.clone.clone.1 | custom fusion | flops 2097152 | bytes 25166080 | tf_op jit(solution)/shard_map/while/body/eval_jaxpr/scatter-add | solution.py:25
  203.3 138.4 %reduce-scatter.3.cloned.1.call-done = f32[256,256]{1,0:T(8,128)} async-done(((f32[8192,256]{1,0:T(8,128)}), f32[256,256]{1,0:T(8,128)}) %reduce-scatter.3.cloned.1.call-update) | async-done | bytes 262160 | tf_op jit(solution)/shard_map/reduce_scatter | solution.py:48
  344.6 12.0 %copy.11 = bf16[1,1,256,128,128]{3,4,2,1,0:T(8,128)(2,1)} copy(bf16[1,1,256,128,128]{4,3,2,1,0:T(8,128)(2,1)} %bitcast.18) | data formatting | bytes 16777216 | tf_op args[1]
  357.6 65.8 %all-gather.5.cloned.1.call-done = bf16[8192,256]{1,0:T(8,128)(2,1)} async-done(((bf16[256,256]{1,0:T(8,128)(2,1)}), bf16[8192,256]{1,0:T(8,128)(2,1)}) %all-gather.5.cloned.1.call-update) | async-done | bytes 4194320 | tf_op jit(solution)/shard_map/all_gather | solution.py:67
  423.6 102.6 %while.29 = (s32[]{:T(128)}, f32[16,128,256]{2,1,0:T(8,128)S(1)}, s32[256]{0:T(256)S(1)}, s32[]{:T(128)}, bf16[256,128,128]{1,2,0:T(8,128)(2,1)}, /*index=5*/s32...) while((s32[]{:T(128)}, f32[16,128,256]{2,1,0:T(8,128)S(1)}, ...), condition=%wide.region_6.7_spmd.clone, body=%wide.region_4.6_spmd.clone.sunk | while | flops 543164096 | bytes 48240816 | solution.py:29
  429.4 7.4 broadcast_select_fusion.5
  436.8 12.4 %scatter_fusion.1 = f32[16,128,256]{2,1,0:T(8,128)S(1)} fusion(f32[16,128,256]{2,1,0:T(8,128)S(1)} %get-tuple-element.505, s32[64]{0:T(128)S(1)} %compare_select_fusion.9, f32[64,128,256]{2,1,0:T(8,128)} %broadcast_select_fusion.5), kind=kCustom, calls=%fused_computation.3.clone.clone.1 | custom fusion | flops 2097152 | bytes 25166080 | tf_op jit(solution)/shard_map/while/body/eval_jaxpr/scatter-add | solution.py:25
  455.0 7.4 broadcast_select_fusion.5
  462.5 12.5 %scatter_fusion.1 = f32[16,128,256]{2,1,0:T(8,128)S(1)} fusion(f32[16,128,256]{2,1,0:T(8,128)S(1)} %get-tuple-element.505, s32[64]{0:T(128)S(1)} %compare_select_fusion.9, f32[64,128,256]{2,1,0:T(8,128)} %broadcast_select_fusion.5), kind=kCustom, calls=%fused_computation.3.clone.clone.1 | custom fusion | flops 2097152 | bytes 25166080 | tf_op jit(solution)/shard_map/while/body/eval_jaxpr/scatter-add | solution.py:25
  480.7 7.4 broadcast_select_fusion.5
  488.2 12.4 %scatter_fusion.1 = f32[16,128,256]{2,1,0:T(8,128)S(1)} fusion(f32[16,128,256]{2,1,0:T(8,128)S(1)} %get-tuple-element.505, s32[64]{0:T(128)S(1)} %compare_select_fusion.9, f32[64,128,256]{2,1,0:T(8,128)} %broadcast_select_fusion.5), kind=kCustom, calls=%fused_computation.3.clone.clone.1 | custom fusion | flops 2097152 | bytes 25166080 | tf_op jit(solution)/shard_map/while/body/eval_jaxpr/scatter-add | solution.py:25
  506.3 7.4 broadcast_select_fusion.5
  513.8 12.4 %scatter_fusion.1 = f32[16,128,256]{2,1,0:T(8,128)S(1)} fusion(f32[16,128,256]{2,1,0:T(8,128)S(1)} %get-tuple-element.505, s32[64]{0:T(128)S(1)} %compare_select_fusion.9, f32[64,128,256]{2,1,0:T(8,128)} %broadcast_select_fusion.5), kind=kCustom, calls=%fused_computation.3.clone.clone.1 | custom fusion | flops 2097152 | bytes 25166080 | tf_op jit(solution)/shard_map/while/body/eval_jaxpr/scatter-add | solution.py:25
  528.1 76.1 %psum.15 = f32[256]{0:T(256)S(1)} all-reduce(f32[256]{0:T(256)S(1)} %get-tuple-element.355), channel_id=1, replica_groups=mesh['row'=8,'col'=32] {'row','col'}, use_global_device_ids=true, to_apply=%region_10.11 | all-reduce | flops 256 | bytes 2048 | tf_op jit(solution)/shard_map/psum | solution.py:60
  604.8 74.2 %all-reduce.2.cloned.1.call-done = f32[256,256]{1,0:T(8,128)} async-done(((f32[256,256]{1,0:T(8,128)}), f32[256,256]{1,0:T(8,128)}) %all-reduce.2.cloned.1.call-update) | async-done | bytes 262160 | tf_op jit(solution)/shard_map/psum | solution.py:60
  680.7 96.3 %reduce-scatter.5.cloned.1.call-done = f32[2048,32]{0,1:T(8,128)} async-done(((f32[2048,256]{0,1:T(8,128)}), f32[2048,32]{0,1:T(8,128)}) %reduce-scatter.5.cloned.1.call-update) | async-done | bytes 262160 | tf_op jit(solution)/shard_map/reduce_scatter | solution.py:73
  (62 shorter events, 61.8 us)
Async XLA Ops:
  7.2 334.6 %copy-start = (bf16[256,256]{1,0:T(8,128)(2,1)S(1)}, bf16[256,256]{1,0:T(8,128)(2,1)}, u32[]{:S(2)}) copy-start(bf16[256,256]{1,0:T(8,128)(2,1)} %param.15) | copy-start | bytes 393220
  7.2 68.4 %all-gather.3.cloned.1.call-start = ((), (), s32[]{:S(2)}) async-start(), calls=%async_computation.2 | async-start | bytes 1179648 | tf_op jit(solution)/shard_map/all_gather | solution.py:40
  7.9 333.8 %reduce-scatter.3.cloned.1.call-start = ((), (), s32[]{:S(2)}) async-start(), calls=%async_computation.3 | async-start | bytes 8650752 | tf_op jit(solution)/shard_map/reduce_scatter | solution.py:48
  203.3 138.5 %copy-start.2 = (bf16[256,256]{1,0:T(8,128)(2,1)S(1)}, bf16[256,256]{1,0:T(8,128)(2,1)}, u32[]{:S(2)}) copy-start(bf16[256,256]{1,0:T(8,128)(2,1)} %param.17) | copy-start | bytes 393220
  203.3 138.5 %copy-start.3 = (f32[256]{0:T(256)S(1)}, f32[256]{0:T(256)}, u32[]{:S(2)}) copy-start(f32[256]{0:T(256)} %param.16) | copy-start | bytes 3076
  203.3 220.1 %all-gather.5.cloned.1.call-start = ((), (), s32[]{:S(2)}) async-start(), calls=%async_computation.4 | async-start | bytes 4325376 | tf_op jit(solution)/shard_map/all_gather | solution.py:67
  344.5 12.1 %copy-start.1 = (f32[256,256]{1,0:T(8,128)S(1)}, f32[256,256]{1,0:T(8,128)}, u32[]{:S(2)}) copy-start(f32[256,256]{1,0:T(8,128)} %reduce-scatter.3.cloned.1.call-done) | copy-start | bytes 786436
  344.5 334.4 %all-reduce.2.cloned.1.call-start = ((), (), s32[]{:S(2)}) async-start(), calls=%async_computation.6 | async-start | bytes 524288 | tf_op jit(solution)/shard_map/psum | solution.py:60
  357.5 419.4 %reduce-scatter.5.cloned.1.call-start = ((), (), s32[]{:S(2)}) async-start(), calls=%async_computation.5 | async-start | bytes 2359296 | tf_op jit(solution)/shard_map/reduce_scatter | solution.py:73
Sparse Core Ops, SparseCore 0:
  10.6 64.8 all-gather.2
  203.4 138.2 reduce-scatter.2
  344.7 78.7 all-gather.4
  429.3 249.6 all-reduce.1
  682.9 93.9 reduce-scatter.4
where the time goes:
time: 787 us; the launch traced here: 785 us
  waiting for transfers between devices  442 us (56%)
  other arithmetic  138 us (18%)
  blocking collectives  76.1 us (10%)
  matrix products  62.7 us (8%)
  local copies, waits for them, and re-layouts  51.5 us (7%)
  between operations  13.8 us (2%)
    reduce_scatter x1, waiting for transfers between devices, on_device(): lax.psum_scatter(partial_value, 'col', scatter_dimension=0, tiled=True)  138 us
    scatter-add x8, other arithmetic, one_group(): return totals.at[put_to].add(products)  128 us
    reduce_scatter x1, waiting for transfers between devices, on_device(): lax.psum_scatter(partial_x, 'row', scatter_dimension=1, tiled=True)  96.3 us
    psum x1, blocking collectives, on_device(): weight_sum, bias_sum = lax.psum((weight_term, bias_term), ('row', 'col'))  76.1 us
    psum x1, waiting for transfers between devices, on_device(): weight_sum, bias_sum = lax.psum((weight_term, bias_term), ('row', 'col'))  74.2 us
    all_gather x1, waiting for transfers between devices, on_device(): feat_tile = lax.all_gather(features, 'row', axis=1, tiled=True)  66.8 us
    all_gather x1, waiting for transfers between devices, on_device(): grad_tile = lax.all_gather(grad_agg, 'col', axis=0, tiled=True)  65.8 us
    dot_general x8, matrix products, one_group(): jnp.einsum(pattern, slab_vals, picked, preferred_element_type=jnp.float32)  59 us
  transfers between devices with their start and end apart: 5, of which 5 were waited for; matrix products, arithmetic and copies ran while one was open for 15% of the time, Pallas kernels for 0%

commit v1 on v0

--- a/solution.py
+++ b/solution.py
@@ -64,7 +64,15 @@
     grad_agg = lax.dot_general(
         grad_pre, weight, (((1,), (1,)), ((), ())), preferred_element_type=jnp.float32
     ).astype(jnp.bfloat16)
-    grad_tile = lax.all_gather(grad_agg, "col", axis=0, tiled=True)
+    grad_tile = jnp.concatenate(
+        jax.lax.all_to_all(
+            jnp.stack([grad_agg for _ in range(jax.lax.axis_size("col"))], axis=0),
+            axis_name="col",
+            split_axis=0,
+            concat_axis=0,
+        ),
+        0,
+    )
     grad_blocks = grad_tile.reshape(row_blocks, block_size, feat_width)
     partial_x = block_products(
         block_vals, grad_blocks, col_ids, row_ids, live_count, col_blocks, True

time: 787 us -> 752 us (0.956)
  waiting for transfers between devices: 442 us -> 382 us
  starting transfers between devices: 0.2 us -> 25 us
    all_to_all x0 -> x1, waiting for transfers between devices: none -> 81 us  [on_device(): jax.lax.all_to_all(jnp.stack([grad_agg for _ in range(jax.lax.axis_size('...]
    psum x1, waiting for transfers between devices: 74.2 us -> 0.01 us  [on_device(): weight_sum, bias_sum = lax.psum((weight_term, bias_term), ('row', 'col'))]
    all_gather x1 -> x0, waiting for transfers between devices: 65.8 us -> none  [on_device(): grad_tile = lax.all_gather(grad_agg, 'col', axis=0, tiled=True)]
    all_to_all x0 -> x1, starting transfers between devices: none -> 24.9 us  [on_device(): jax.lax.all_to_all(jnp.stack([grad_agg for _ in range(jax.lax.axis_size('...]
  transfers between devices with their start and end apart: 5 -> 5, of which waited for: 5 -> 4; matrix products, arithmetic and copies ran while one was open for 15% -> 16% of each run, Pallas kernels for 0% -> 0%
where the time goes in v1:
time: 752 us; the launch traced here: 750 us
  waiting for transfers between devices  382 us (51%)
  other arithmetic  138 us (18%)
  blocking collectives  75 us (10%)
  matrix products  62 us (8%)
  local copies, waits for them, and re-layouts  53.8 us (7%)
  starting transfers between devices  25 us (3%)
  between operations  13.8 us (2%)
    reduce_scatter x1, waiting for transfers between devices, on_device(): lax.psum_scatter(partial_value, 'col', scatter_dimension=0, tiled=True)  139 us
    scatter-add x8, other arithmetic, one_group(): return totals.at[put_to].add(products)  128 us
    reduce_scatter x1, waiting for transfers between devices, on_device(): lax.psum_scatter(partial_x, 'row', scatter_dimension=1, tiled=True)  95 us
    all_to_all x1, waiting for transfers between devices, on_device(): jax.lax.all_to_all(jnp.stack([grad_agg for _ in range(jax.lax.axis_size('...  81 us
    psum x1, blocking collectives, on_device(): weight_sum, bias_sum = lax.psum((weight_term, bias_term), ('row', 'col'))  75 us
    all_gather x1, waiting for transfers between devices, on_device(): feat_tile = lax.all_gather(features, 'row', axis=1, tiled=True)  66.8 us
    dot_general x8, matrix products, one_group(): jnp.einsum(pattern, slab_vals, picked, preferred_element_type=jnp.float32)  59 us
    gather x8, local copies, waits for them, and re-layouts, one_group(): picked = jnp.take(source, take_from, axis=0)  30.9 us
  transfers between devices with their start and end apart: 5, of which 4 were waited for; matrix products, arithmetic and copies ran while one was open for 16% of the time, Pallas kernels for 0%

profile of v1, /device:TPU:2, one launch (start us, length us, event | category | flops | bytes accessed | tf_op | source)
XLA Modules:
  0.0 750.5 jit_solution(5487249238387106441)
XLA Ops:
  8.7 66.8 %all-gather.2.cloned.1.call-done = bf16[2048,256]{0,1:T(8,128)(2,1)} async-done(((bf16[2048,32]{0,1:T(8,128)(2,1)}), bf16[2048,256]{0,1:T(8,128)(2,1)}) %all-gather.2.cloned.1.call-update) | async-done | bytes 1048592 | tf_op jit(solution)/shard_map/all_gather | solution.py:40
  81.3 122.0 %while.28 = (s32[]{:T(128)}, f32[64,128,256]{2,1,0:T(8,128)}, s32[256]{0:T(256)S(1)}, s32[]{:T(128)}, bf16[256,128,128]{2,1,0:T(8,128)(2,1)}, /*index=5*/s32[256...) while((s32[]{:T(128)}, f32[64,128,256]{2,1,0:T(8,128)}, ...), condition=%wide.region_2.3_spmd.clone, body=%wide.region_0.2_spmd.clone.sunk | while | flops 543164096 | bytes 48240816 | solution.py:29
  84.7 7.4 broadcast_select_fusion.4
  92.2 19.6 %scatter_fusion = f32[64,128,256]{2,1,0:T(8,128)} fusion(f32[64,128,256]{2,1,0:T(8,128)} %get-tuple-element.472, s32[64]{0:T(128)S(1)} %compare_select_fusion.8, f32[64,128,256]{2,1,0:T(8,128)} %broadcast_select_fusion.4), kind=kCustom, calls=%fused_computation.2.clone.clone.1 | custom fusion | flops 2097152 | bytes 25166080 | tf_op jit(solution)/shard_map/while/body/eval_jaxpr/scatter-add | solution.py:25
  122.8 19.4 %scatter_fusion = f32[64,128,256]{2,1,0:T(8,128)} fusion(f32[64,128,256]{2,1,0:T(8,128)} %get-tuple-element.472, s32[64]{0:T(128)S(1)} %compare_select_fusion.8, f32[64,128,256]{2,1,0:T(8,128)} %broadcast_select_fusion.4), kind=kCustom, calls=%fused_computation.2.clone.clone.1 | custom fusion | flops 2097152 | bytes 25166080 | tf_op jit(solution)/shard_map/while/body/eval_jaxpr/scatter-add | solution.py:25
  145.7 7.4 broadcast_select_fusion.4
  153.1 19.6 %scatter_fusion = f32[64,128,256]{2,1,0:T(8,128)} fusion(f32[64,128,256]{2,1,0:T(8,128)} %get-tuple-element.472, s32[64]{0:T(128)S(1)} %compare_select_fusion.8, f32[64,128,256]{2,1,0:T(8,128)} %broadcast_select_fusion.4), kind=kCustom, calls=%fused_computation.2.clone.clone.1 | custom fusion | flops 2097152 | bytes 25166080 | tf_op jit(solution)/shard_map/while/body/eval_jaxpr/scatter-add | solution.py:25
  176.2 7.4 broadcast_select_fusion.4
  183.6 19.6 %scatter_fusion = f32[64,128,256]{2,1,0:T(8,128)} fusion(f32[64,128,256]{2,1,0:T(8,128)} %get-tuple-element.472, s32[64]{0:T(128)S(1)} %compare_select_fusion.8, f32[64,128,256]{2,1,0:T(8,128)} %broadcast_select_fusion.4), kind=kCustom, calls=%fused_computation.2.clone.clone.1 | custom fusion | flops 2097152 | bytes 25166080 | tf_op jit(solution)/shard_map/while/body/eval_jaxpr/scatter-add | solution.py:25
  203.3 138.8 %reduce-scatter.3.cloned.1.call-done = f32[256,256]{1,0:T(8,128)} async-done(((f32[8192,256]{1,0:T(8,128)}), f32[256,256]{1,0:T(8,128)}) %reduce-scatter.3.cloned.1.call-update) | async-done | bytes 262160 | tf_op jit(solution)/shard_map/reduce_scatter | solution.py:48
  346.6 24.9 %all-to-all-start = ((bf16[32,256,256]{2,1,0:T(8,128)(2,1)}), bf16[32,256,256]{2,1,0:T(8,128)(2,1)}, u32[]{:S(2)}, u32[]{:S(2)}) async-start(bf16[32,256,256]{2,1,0:T(8,128)(2,1)} %stack.2), calls=%async_computation.1 | async-start | bytes 8388608 | tf_op jit(solution)/shard_map/all_to_all | solution.py:68
  371.5 12.0 %copy.11 = bf16[1,1,256,128,128]{3,4,2,1,0:T(8,128)(2,1)} copy(bf16[1,1,256,128,128]{4,3,2,1,0:T(8,128)(2,1)} %bitcast.17) | data formatting | bytes 16777216 | tf_op args[1]
  384.5 81.0 %all-to-all-done = bf16[32,256,256]{2,1,0:T(8,128)(2,1)} async-done(((bf16[32,256,256]{2,1,0:T(8,128)(2,1)}), bf16[32,256,256]{2,1,0:T(8,128)(2,1)}, u32[]{:S(2)}, u32[]{:S(2)}) %all-to-all-start) | async-done | bytes 4194336 | tf_op jit(solution)/shard_map/all_to_all | solution.py:68
  465.7 102.5 %while.29 = (s32[]{:T(128)}, f32[16,128,256]{2,1,0:T(8,128)S(1)}, s32[256]{0:T(256)S(1)}, s32[]{:T(128)}, bf16[256,128,128]{1,2,0:T(8,128)(2,1)}, /*index=5*/s32...) while((s32[]{:T(128)}, f32[16,128,256]{2,1,0:T(8,128)S(1)}, ...), condition=%wide.region_6.7_spmd.clone, body=%wide.region_4.6_spmd.clone.sunk | while | flops 543164096 | bytes 48240816 | solution.py:29
  471.5 7.4 broadcast_select_fusion.5
  478.9 12.4 %scatter_fusion.1 = f32[16,128,256]{2,1,0:T(8,128)S(1)} fusion(f32[16,128,256]{2,1,0:T(8,128)S(1)} %get-tuple-element.505, s32[64]{0:T(128)S(1)} %compare_select_fusion.9, f32[64,128,256]{2,1,0:T(8,128)} %broadcast_select_fusion.5), kind=kCustom, calls=%fused_computation.3.clone.clone.1 | custom fusion | flops 2097152 | bytes 25166080 | tf_op jit(solution)/shard_map/while/body/eval_jaxpr/scatter-add | solution.py:25
  497.1 7.4 broadcast_select_fusion.5
  504.6 12.4 %scatter_fusion.1 = f32[16,128,256]{2,1,0:T(8,128)S(1)} fusion(f32[16,128,256]{2,1,0:T(8,128)S(1)} %get-tuple-element.505, s32[64]{0:T(128)S(1)} %compare_select_fusion.9, f32[64,128,256]{2,1,0:T(8,128)} %broadcast_select_fusion.5), kind=kCustom, calls=%fused_computation.3.clone.clone.1 | custom fusion | flops 2097152 | bytes 25166080 | tf_op jit(solution)/shard_map/while/body/eval_jaxpr/scatter-add | solution.py:25
  522.7 7.4 broadcast_select_fusion.5
  530.2 12.4 %scatter_fusion.1 = f32[16,128,256]{2,1,0:T(8,128)S(1)} fusion(f32[16,128,256]{2,1,0:T(8,128)S(1)} %get-tuple-element.505, s32[64]{0:T(128)S(1)} %compare_select_fusion.9, f32[64,128,256]{2,1,0:T(8,128)} %broadcast_select_fusion.5), kind=kCustom, calls=%fused_computation.3.clone.clone.1 | custom fusion | flops 2097152 | bytes 25166080 | tf_op jit(solution)/shard_map/while/body/eval_jaxpr/scatter-add | solution.py:25
  548.4 7.4 broadcast_select_fusion.5
  555.8 12.4 %scatter_fusion.1 = f32[16,128,256]{2,1,0:T(8,128)S(1)} fusion(f32[16,128,256]{2,1,0:T(8,128)S(1)} %get-tuple-element.505, s32[64]{0:T(128)S(1)} %compare_select_fusion.9, f32[64,128,256]{2,1,0:T(8,128)} %broadcast_select_fusion.5), kind=kCustom, calls=%fused_computation.3.clone.clone.1 | custom fusion | flops 2097152 | bytes 25166080 | tf_op jit(solution)/shard_map/while/body/eval_jaxpr/scatter-add | solution.py:25
  570.1 75.0 %psum.15 = f32[256]{0:T(256)S(1)} all-reduce(f32[256]{0:T(256)S(1)} %get-tuple-element.355), channel_id=1, replica_groups=mesh['row'=8,'col'=32] {'row','col'}, use_global_device_ids=true, to_apply=%region_10.11 | all-reduce | flops 256 | bytes 2048 | tf_op jit(solution)/shard_map/psum | solution.py:60
  647.3 95.0 %reduce-scatter.5.cloned.1.call-done = f32[2048,32]{0,1:T(8,128)} async-done(((f32[2048,256]{0,1:T(8,128)}), f32[2048,32]{0,1:T(8,128)}) %reduce-scatter.5.cloned.1.call-update) | async-done | bytes 262160 | tf_op jit(solution)/shard_map/reduce_scatter | solution.py:81
  (64 shorter events, 63.5 us)
Async XLA Ops:
  7.2 334.9 %copy-start = (bf16[256,256]{1,0:T(8,128)(2,1)S(1)}, bf16[256,256]{1,0:T(8,128)(2,1)}, u32[]{:S(2)}) copy-start(bf16[256,256]{1,0:T(8,128)(2,1)} %param.15) | copy-start | bytes 393220
  7.2 68.4 %all-gather.2.cloned.1.call-start = ((), (), s32[]{:S(2)}) async-start(), calls=%async_computation.3 | async-start | bytes 1179648 | tf_op jit(solution)/shard_map/all_gather | solution.py:40
  7.9 334.1 %reduce-scatter.3.cloned.1.call-start = ((), (), s32[]{:S(2)}) async-start(), calls=%async_computation.4 | async-start | bytes 8650752 | tf_op jit(solution)/shard_map/reduce_scatter | solution.py:48
  203.3 138.8 %copy-start.3 = (bf16[256,256]{1,0:T(8,128)(2,1)S(1)}, bf16[256,256]{1,0:T(8,128)(2,1)}, u32[]{:S(2)}) copy-start(bf16[256,256]{1,0:T(8,128)(2,1)} %param.17) | copy-start | bytes 393220
  203.3 138.8 %copy-start.4 = (f32[256]{0:T(256)S(1)}, f32[256]{0:T(256)}, u32[]{:S(2)}) copy-start(f32[256]{0:T(256)} %param.16) | copy-start | bytes 3076
  346.6 118.9 %all-to-all-start = ((bf16[32,256,256]{2,1,0:T(8,128)(2,1)}), bf16[32,256,256]{2,1,0:T(8,128)(2,1)}, u32[]{:S(2)}, u32[]{:S(2)}) async-start(bf16[32,256,256]{2,1,0:T(8,128)(2,1)} %stack.2), calls=%async_computation.1 | async-start | bytes 8388608 | tf_op jit(solution)/shard_map/all_to_all | solution.py:68
  371.5 12.1 %copy-start.2 = (f32[256,256]{1,0:T(8,128)S(1)}, f32[256,256]{1,0:T(8,128)}, u32[]{:S(2)}) copy-start(f32[256,256]{1,0:T(8,128)} %reduce-scatter.3.cloned.1.call-done) | copy-start | bytes 786436
  371.5 274.2 %all-reduce.2.cloned.1.call-start = ((), (), s32[]{:S(2)}) async-start(), calls=%async_computation.6 | async-start | bytes 524288 | tf_op jit(solution)/shard_map/psum | solution.py:60
  384.5 357.8 %reduce-scatter.5.cloned.1.call-start = ((), (), s32[]{:S(2)}) async-start(), calls=%async_computation.5 | async-start | bytes 2359296 | tf_op jit(solution)/shard_map/reduce_scatter | solution.py:81
  568.2 175.7 %copy-start.1 = (bf16[256,256]{1,0:T(8,128)(2,1)S(1)}, bf16[256,256]{1,0:T(8,128)(2,1)}, u32[]{:S(2)}) copy-start(bf16[256,256]{1,0:T(8,128)(2,1)} %param.15) | copy-start | bytes 393220
Sparse Core Ops, SparseCore 0:
  10.6 64.8 all-gather.1
  203.4 138.6 reduce-scatter.2
  384.6 259.6 all-reduce.1
  648.2 94.0 reduce-scatter.4
